TPU v7x, 32 devices: a whole 2x2x4 slice. The times are simulated.
32 devices in a mesh: frames: 8 (over z, x), heads: 4 (over y, core).
Axes of the slice: x: 2, y: 2, z: 4, core: 2. Of those that a mesh axis runs over, the one named last changes fastest.
Arguments:
- queries: bfloat16 [1024, 4096], P('frames', 'heads'), may hold values from -9 to 9
- keys: bfloat16 [1024, 512], P(('frames', 'heads')), may hold values from -4.5 to 4.5
- values: bfloat16 [1024, 512], P(('frames', 'heads')), may hold values from -6 to 6
- block_mask: int32 [8, 8], replicated, may hold values from 0 to 1, as said below
- lengths: int32 [8], replicated, may hold values from 64 to 128, as said below
Outputs:
- attended: bfloat16 [1024, 4096], P('frames', 'heads')
Inputs may be any that keep to these rules, and one draw needn't show every extreme that they name: block_mask[i, i] = 1 and block_mask[i, j] = 0 for j > i. `lengths`: some frame group is full in every draw.
All inputs are finite; a program needn't handle non-finite values.
Results may differ from a plain program's by a relative error of at most 0.0055.
Values may be sent and summed in bfloat16 or wider, within the bound.
A program may use at most 64 MiB of HBM per device.

v0:
```python
import math
import jax
import jax.numpy as jnp
from jax import lax
from jax.sharding import PartitionSpec as P

HEAD_DIM = 128
masked_score = -1e30


def attend(query_sets, keys_mine, values_mine, block_mask, lengths, group_tokens):
    kv_local = keys_mine.shape[1] // HEAD_DIM
    q_local = query_sets[0][0].shape[1] // HEAD_DIM
    per_kv = q_local // kv_local
    scale = HEAD_DIM ** (-0.5)
    group_count = block_mask.shape[0]
    group_ids = jnp.arange(group_count, dtype=jnp.int32)
    prepared = []
    initial = []
    for rows, owner in query_sets:
        count = rows.shape[0]
        prepared.append(
            (
                rows.reshape(count, kv_local, per_kv, HEAD_DIM),
                lax.dynamic_slice_in_dim(block_mask, owner, 1, 0)[0],
            )
        )
        initial.append(
            (
                jnp.full((kv_local, per_kv, count), masked_score, jnp.float32),
                jnp.zeros((kv_local, per_kv, count), jnp.float32),
                jnp.zeros((count, kv_local, per_kv, HEAD_DIM), jnp.float32),
            )
        )
    key_piece = lax.all_gather(keys_mine, "frames", axis=0, tiled=True)
    value_piece = lax.all_gather(values_mine, "frames", axis=0, tiled=True)
    fold_rows = key_piece.shape[0]
    width = math.gcd(fold_rows, 512)
    blocks = fold_rows // width
    key_blocks = key_piece.reshape(blocks, width, kv_local, HEAD_DIM)
    value_blocks = value_piece.reshape(blocks, width, kv_local, HEAD_DIM)

    def one_block(state, inputs):
        key_block, value_block, number = inputs
        positions = number * width + jnp.arange(width, dtype=jnp.int32)
        key_group = positions // group_tokens
        within = positions % group_tokens
        onehot = (key_group[:, None] == group_ids[None, :]).astype(jnp.int32)
        live_len = jnp.sum(onehot * lengths[None, :], axis=1)
        updated = []
        for (query_rows, mask_row), (running_max, running_total, running_acc) in zip(
            prepared, state
        ):
            allowed = jnp.sum(onehot * mask_row[None, :], axis=1)
            valid = (allowed > 0) & (within < live_len)

            def update(current):
                old_max, old_total, old_acc = current
                scores = (
                    jnp.einsum(
                        "tkgd,skd->kgts", query_rows, key_block, preferred_element_type=jnp.float32
                    )
                    * scale
                )
                scores = jnp.where(valid[None, None, None, :], scores, masked_score)
                new_max = jnp.maximum(old_max, jnp.max(scores, axis=-1))
                probs = jnp.exp(scores - new_max[..., None])
                factor = jnp.exp(old_max - new_max)
                new_total = old_total * factor + jnp.sum(probs, axis=-1)
                added = jnp.einsum(
                    "kgts,skd->tkgd",
                    probs.astype(jnp.bfloat16),
                    value_block,
                    preferred_element_type=jnp.float32,
                )
                new_acc = old_acc * jnp.transpose(factor, (2, 0, 1))[..., None] + added
                return (new_max, new_total, new_acc)

            updated.append(
                lax.cond(
                    jnp.any(valid),
                    update,
                    lambda current: current,
                    (running_max, running_total, running_acc),
                )
            )
        return (tuple(updated), None)

    numbers = jnp.arange(blocks, dtype=jnp.int32)
    final, unused = lax.scan(one_block, tuple(initial), (key_blocks, value_blocks, numbers))
    results = []
    for (rows, owner), (running_max, running_total, running_acc) in zip(query_sets, final):
        output = running_acc / jnp.transpose(running_total, (2, 0, 1))[..., None]
        results.append(output.astype(jnp.bfloat16).reshape(rows.shape[0], q_local * HEAD_DIM))
    return results


def local(queries, keys, values, block_mask, lengths):
    keys_mine, values_mine = (
        lax.all_to_all(keys, "heads", split_axis=1, concat_axis=0, tiled=True),
        lax.all_to_all(values, "heads", split_axis=1, concat_axis=0, tiled=True),
    )
    group_tokens = queries.shape[0]
    frame_index = lax.axis_index("frames")
    outputs = attend(
        [(queries, frame_index)], keys_mine, values_mine, block_mask, lengths, group_tokens
    )
    return outputs[0]


def solution(mesh):
    return jax.shard_map(
        local,
        mesh=mesh,
        in_specs=(
            P("frames", "heads"),
            P(("frames", "heads"), None),
            P(("frames", "heads"), None),
            P(),
            P(),
        ),
        out_specs=P("frames", "heads"),
        check_vma=False,
    )
```

profile of v0, /device:TPU:30, one launch (start us, length us, event | category | flops | bytes accessed | tf_op | source)
XLA Modules:
  0.0 84.3 jit_solution(984634713009666700)
XLA Ops:
  0.0 0.8 copy-done
  0.8 0.6 copy_bitcast_fusion
  1.4 3.7 %all-to-all-start.1 = ((bf16[32,4,128]{2,0,1:T(8,128)(2,1)}), bf16[32,4,128]{2,0,1:T(8,128)(2,1)S(1)}, u32[]{:S(2)}, u32[]{:S(2)}) async-start(bf16[32,4,128]{2,0,1:T(8,128)(2,1)} %copy_bitcast_fusion), calls=%async_computation.1 | async-start | bytes 65536 | tf_op jit(solution)/shard_map/all_to_all | solution.py:101
  5.1 1.4 %copy_bitcast_fusion.1 = bf16[32,4,128]{2,0,1:T(8,128)(2,1)} fusion(bf16[32,512]{1,0:T(8,128)(2,1)} %param.10), kind=kLoop, calls=%fused_computation.47 | loop fusion | bytes 65536 | tf_op jit(solution)/shard_map/all_to_all | solution.py:100
  6.5 0.7 constant_dynamic-slice_fusion
  7.2 1.1 %copy.37 = bf16[128,1024]{0,1:T(8,128)(2,1)S(1)} copy(bf16[128,1024]{1,0:T(8,128)(2,1)} %param.9) | data formatting | bytes 524288 | tf_op args[0]
  8.3 0.2 copy.39
  8.5 3.8 %all-to-all-start = ((bf16[32,4,128]{2,0,1:T(8,128)(2,1)}), bf16[32,4,128]{2,0,1:T(8,128)(2,1)S(1)}, u32[]{:S(2)}, u32[]{:S(2)}) async-start(bf16[32,4,128]{2,0,1:T(8,128)(2,1)} %copy_bitcast_fusion.1), calls=%async_computation | async-start | bytes 65536 | tf_op jit(solution)/shard_map/all_to_all | solution.py:100
  12.3 30.8 %all_gather.7 = bf16[1024,128]{1,0:T(8,128)(2,1)S(1)} all-gather(bf16[128,128]{1,0:T(8,128)(2,1)S(1)} %bitcast.97), channel_id=1, replica_groups=mesh['frames'=8,'heads'=4] {'frames'}, dimensions={0}, use_global_device_ids=true | all-gather | bytes 294912 | tf_op jit(solution)/shard_map/all_gather | solution.py:36
  43.3 30.7 %all_gather.6 = bf16[1024,128]{1,0:T(8,128)(2,1)S(1)} all-gather(bf16[128,128]{1,0:T(8,128)(2,1)S(1)} %bitcast.98), channel_id=1, replica_groups=mesh['frames'=8,'heads'=4] {'frames'}, dimensions={0}, use_global_device_ids=true | all-gather | bytes 294912 | tf_op jit(solution)/shard_map/all_gather | solution.py:35
  74.1 9.3 %while.17 = (s32[]{:T(128)}, f32[1,8,128]{2,1,0:T(8,128)S(1)}, f32[1,8,128]{2,1,0:T(8,128)S(1)}, f32[128,1,8,128]{0,3,2,1:T(8,128)S(1)}, s32[2]{0:T(128)S(1)}, /...) while((s32[]{:T(128)}, f32[1,8,128]{2,1,0:T(8,128)S(1)}, ...), condition=%wide.region_8.9_spmd.clone, body=%wide.region_0.8_spmd.clone.sunk | while | flops 274503680 | bytes 7944539 | solution.py:90
  74.1 0.6 dynamic_slice.43
  75.4 0.7 fusion.39
  76.9 1.9 %conditional.3 = ((f32[1,8,128]{2,1,0:T(8,128)S(1)}, f32[1,8,128]{2,1,0:T(8,128)S(1)}, f32[128,1,8,128]{0,3,2,1:T(8,128)S(1)})) conditional(s32[]{:T(128)} %convert_element_type.23, (f32[1,8,128]{2,1,0:T(8,128)S(1)}, f32[1,8,128]{2,1,0:T(8,128)S(1)}, f32[128,1,8,128]{0,3,2,1:T(8,128)S(1)}) %tuple.59, (pred[512]{0:T(512)(128)(4,1)S(1)}, ...), branch_computations={%region_4.4_spmd, %region_5.7_spmd} | conditional | flops 274467840 | bytes 7931432 | solution.py:80
  76.9 0.5 bitcast_reduce_fusion
  77.4 0.8 fusion.5
  78.2 0.5 fusion.4
  78.7 0.6 dynamic_slice.43
  80.1 0.7 fusion.39
  81.5 1.9 %conditional.3 = ((f32[1,8,128]{2,1,0:T(8,128)S(1)}, f32[1,8,128]{2,1,0:T(8,128)S(1)}, f32[128,1,8,128]{0,3,2,1:T(8,128)S(1)})) conditional(s32[]{:T(128)} %convert_element_type.23, (f32[1,8,128]{2,1,0:T(8,128)S(1)}, f32[1,8,128]{2,1,0:T(8,128)S(1)}, f32[128,1,8,128]{0,3,2,1:T(8,128)S(1)}) %tuple.59, (pred[512]{0:T(512)(128)(4,1)S(1)}, ...), branch_computations={%region_4.4_spmd, %region_5.7_spmd} | conditional | flops 274467840 | bytes 7931432 | solution.py:80
  81.5 0.5 bitcast_reduce_fusion
  82.0 0.8 fusion.5
  82.9 0.5 fusion.4
  83.5 0.9 %copy.43 = bf16[128,1024]{1,0:T(8,128)(2,1)} copy(bf16[128,1024]{0,1:T(8,128)(2,1)S(1)} %bitcast.93) | data formatting | bytes 524288 | tf_op jit(solution)/shard_map/reshape | solution.py:94
  (21 shorter events, 0.5 us)
Async XLA Ops:
  0.0 0.8 copy-start
  0.8 73.3 %copy-start.1 = (s32[8]{0:T(128)S(1)}, s32[8]{0:T(128)}, u32[]{:S(2)}) copy-start(s32[8]{0:T(128)} %param.13) | copy-start | bytes 100
  1.4 7.1 %all-to-all-start.1 = ((bf16[32,4,128]{2,0,1:T(8,128)(2,1)}), bf16[32,4,128]{2,0,1:T(8,128)(2,1)S(1)}, u32[]{:S(2)}, u32[]{:S(2)}) async-start(bf16[32,4,128]{2,0,1:T(8,128)(2,1)} %copy_bitcast_fusion), calls=%async_computation.1 | async-start | bytes 65536 | tf_op jit(solution)/shard_map/all_to_all | solution.py:101
  8.5 34.8 %all-to-all-start = ((bf16[32,4,128]{2,0,1:T(8,128)(2,1)}), bf16[32,4,128]{2,0,1:T(8,128)(2,1)S(1)}, u32[]{:S(2)}, u32[]{:S(2)}) async-start(bf16[32,4,128]{2,0,1:T(8,128)(2,1)} %copy_bitcast_fusion.1), calls=%async_computation | async-start | bytes 65536 | tf_op jit(solution)/shard_map/all_to_all | solution.py:100
where the time goes:
time: 84.8 us; the launch traced here: 84.3 us
  blocking collectives  61.6 us (73%)
  starting transfers between devices  7.53 us (9%)
  local copies, waits for them, and re-layouts  6.95 us (8%)
  loops' own time  2.87 us (3%)
  other arithmetic  2.72 us (3%)
  matrix products  2.59 us (3%)
    all_gather x1, blocking collectives, attend(): value_piece = lax.all_gather(values_mine, 'frames', axis=0, tiled=True)  30.8 us
    all_gather x1, blocking collectives, attend(): key_piece = lax.all_gather(keys_mine, 'frames', axis=0, tiled=True)  30.7 us
    all_to_all x1, starting transfers between devices, local(): lax.all_to_all(keys, 'heads', split_axis=1, concat_axis=0, tiled=True)  3.79 us
    all_to_all x1, starting transfers between devices, local(): lax.all_to_all(values, 'heads', split_axis=1, concat_axis=0, tiled=True)  3.74 us
    another operation x1, loops' own time, attend(): lax.scan(one_block, tuple(initial), (key_blocks, value_blocks, numbers))  2.76 us
    unnamed x7, local copies, waits for them, and re-layouts  2.2 us
  transfers between devices with their start and end apart: 2, of which 0 were waited for; matrix products, arithmetic and copies ran while one was open for 4% of the time, Pallas kernels for 0%

commit v1 on v0

--- a/solution.py
+++ b/solution.py
@@ -1,3 +1,4 @@
+import functools
 import math
 import jax
 import jax.numpy as jnp
@@ -6,6 +7,16 @@
 
 HEAD_DIM = 128
 masked_score = -1e30
+
+
+def obtain_the_edge(tile_in, row_dim):
+    z1 = jnp.stack([tile_in] * jax.lax.axis_size("frames"))
+    front = jax.lax.all_to_all(z1, "frames", 0, 0)
+    current_value = jnp.concatenate(front, axis=row_dim)
+    return current_value
+
+
+update_the_limits = functools.partial(obtain_the_edge, row_dim=0)
 
 
 def attend(query_sets, keys_mine, values_mine, block_mask, lengths, group_tokens):
@@ -32,7 +43,7 @@
                 jnp.zeros((count, kv_local, per_kv, HEAD_DIM), jnp.float32),
             )
         )
-    key_piece = lax.all_gather(keys_mine, "frames", axis=0, tiled=True)
+    key_piece = update_the_limits(keys_mine)
     value_piece = lax.all_gather(values_mine, "frames", axis=0, tiled=True)
     fold_rows = key_piece.shape[0]
     width = math.gcd(fold_rows, 512)

time: 84.8 us -> 65 us (0.77)
  the two profiles are of different devices: /device:TPU:30 before, /device:TPU:26 now
where the time goes in v1:
time: 65 us; the launch traced here: 64.4 us
  blocking collectives  37 us (57%)
  starting transfers between devices  9.26 us (14%)
  local copies, waits for them, and re-layouts  7.1 us (11%)
  waiting for transfers between devices  3.15 us (5%)
  loops' own time  2.61 us (4%)
  matrix products  2.59 us (4%)
  other arithmetic  2.55 us (4%)
    all_gather x1, blocking collectives, attend(): value_piece = lax.all_gather(values_mine, 'frames', axis=0, tiled=True)  30.7 us
    all_to_all x1, blocking collectives, local(): lax.all_to_all(keys, 'heads', split_axis=1, concat_axis=0, tiled=True)  6.29 us
    all_to_all x1, starting transfers between devices, obtain_the_edge(): front = jax.lax.all_to_all(z1, 'frames', 0, 0)  6 us
    all_to_all x1, starting transfers between devices, local(): lax.all_to_all(values, 'heads', split_axis=1, concat_axis=0, tiled=True)  3.26 us
    all_to_all x1, waiting for transfers between devices, local(): lax.all_to_all(values, 'heads', split_axis=1, concat_axis=0, tiled=True)  3.14 us
    another operation x1, loops' own time, attend(): lax.scan(one_block, tuple(initial), (key_blocks, value_blocks, numbers))  2.5 us
    unnamed x7, local copies, waits for them, and re-layouts  2.2 us
    dot_general x2, matrix products, update(): jnp.einsum('kgts,skd->tkgd', probs.astype(jnp.bfloat16), value_block, pre...  1.68 us
  transfers between devices with their start and end apart: 2, of which 1 were waited for; matrix products, arithmetic and copies ran while one was open for 5% of the time, Pallas kernels for 0%

profile of v1, /device:TPU:26, one launch (start us, length us, event | category | flops | bytes accessed | tf_op | source)
XLA Modules:
  0.0 64.4 jit_solution(6874277777161926)
XLA Ops:
  0.0 0.8 %copy-done = bf16[32,512]{1,0:T(8,128)(2,1)S(1)} copy-done((bf16[32,512]{1,0:T(8,128)(2,1)S(1)}, bf16[32,512]{1,0:T(8,128)(2,1)}, u32[]{:S(2)}) %copy-start) | copy-done | bytes 32792
  0.8 0.6 copy_bitcast_fusion
  1.4 3.3 %all-to-all-start.2 = ((bf16[32,4,128]{2,0,1:T(8,128)(2,1)}), bf16[32,4,128]{2,0,1:T(8,128)(2,1)S(1)}, u32[]{:S(2)}, u32[]{:S(2)}) async-start(bf16[32,4,128]{2,0,1:T(8,128)(2,1)} %copy_bitcast_fusion), calls=%async_computation.2 | async-start | bytes 65536 | tf_op jit(solution)/shard_map/all_to_all | solution.py:112
  4.7 0.8 %copy_bitcast_fusion.1 = bf16[32,4,128]{2,0,1:T(8,128)(2,1)S(1)} fusion(bf16[32,512]{1,0:T(8,128)(2,1)} %param.10), kind=kLoop, calls=%fused_computation.47 | loop fusion | bytes 65536 | tf_op jit(solution)/shard_map/all_to_all | solution.py:111
  5.4 3.1 %all-to-all-done.2 = bf16[32,4,128]{2,0,1:T(8,128)(2,1)S(1)} async-done(((bf16[32,4,128]{2,0,1:T(8,128)(2,1)}), bf16[32,4,128]{2,0,1:T(8,128)(2,1)S(1)}, u32[]{:S(2)}, u32[]{:S(2)}) %all-to-all-start.2) | async-done | bytes 32800 | tf_op jit(solution)/shard_map/all_to_all | solution.py:112
  8.6 6.3 %all_to_all.40 = bf16[32,4,128]{2,0,1:T(8,128)(2,1)S(1)} all-to-all(bf16[32,4,128]{2,0,1:T(8,128)(2,1)S(1)} %copy_bitcast_fusion.1), channel_id=1, replica_groups=mesh['frames'=8,'heads'=4] {'heads'}, dimensions={1} | all-to-all | bytes 65536 | tf_op jit(solution)/shard_map/all_to_all | solution.py:111
  14.9 0.7 %stack.5 = bf16[8,128,128]{2,1,0:T(8,128)(2,1)} broadcast(bf16[128,128]{1,0:T(8,128)(2,1)S(1)} %bitcast.98), dimensions={1,2} | broadcast | bytes 294912 | tf_op jit(solution)/shard_map/stack | solution.py:13
  15.6 6.0 %all-to-all-start.1 = ((bf16[8,128,128]{2,1,0:T(8,128)(2,1)}), bf16[8,128,128]{2,1,0:T(8,128)(2,1)S(1)}, u32[]{:S(2)}, u32[]{:S(2)}) async-start(bf16[8,128,128]{2,1,0:T(8,128)(2,1)} %stack.5), calls=%async_computation.1 | async-start | bytes 524288 | tf_op jit(solution)/shard_map/all_to_all | solution.py:14
  21.6 1.1 %copy.29 = bf16[128,1024]{0,1:T(8,128)(2,1)S(1)} copy(bf16[128,1024]{1,0:T(8,128)(2,1)} %param.9) | data formatting | bytes 524288 | tf_op args[0]
  22.9 0.7 %constant_dynamic-slice_fusion = s32[1,8]{1,0:T(1,128)S(1)} fusion(s32[8,8]{1,0:T(8,128)} %param.12, s32[]{:T(128)S(6)} %select_n.36), kind=kLoop, calls=%fused_computation.48 | loop fusion | bytes 68 | tf_op jit(solution)/shard_map/dynamic_slice | solution.py:36
  23.6 30.7 %all_gather.3 = bf16[1024,128]{1,0:T(8,128)(2,1)S(1)} all-gather(bf16[128,128]{1,0:T(8,128)(2,1)S(1)} %bitcast.97), channel_id=1, replica_groups=mesh['frames'=8,'heads'=4] {'frames'}, dimensions={0}, use_global_device_ids=true | all-gather | bytes 294912 | tf_op jit(solution)/shard_map/all_gather | solution.py:47
  54.6 8.9 %while.17 = (s32[]{:T(128)}, f32[1,8,128]{2,1,0:T(8,128)S(1)}, f32[1,8,128]{2,1,0:T(8,128)S(1)}, f32[128,1,8,128]{0,3,2,1:T(8,128)S(1)}, s32[2]{0:T(128)S(1)}, /...) while((s32[]{:T(128)}, f32[1,8,128]{2,1,0:T(8,128)S(1)}, ...), condition=%wide.region_8.9_spmd.clone, body=%wide.region_0.8_spmd.clone.sunk | while | flops 274503680 | bytes 7944539 | solution.py:101
  54.6 0.6 dynamic_slice.43
  55.9 0.6 fusion.39
  57.2 1.9 %conditional.3 = ((f32[1,8,128]{2,1,0:T(8,128)S(1)}, f32[1,8,128]{2,1,0:T(8,128)S(1)}, f32[128,1,8,128]{0,3,2,1:T(8,128)S(1)})) conditional(s32[]{:T(128)} %convert_element_type.23, (f32[1,8,128]{2,1,0:T(8,128)S(1)}, f32[1,8,128]{2,1,0:T(8,128)S(1)}, f32[128,1,8,128]{0,3,2,1:T(8,128)S(1)}) %tuple.58, (pred[512]{0:T(512)(128)(4,1)S(1)}, ...), branch_computations={%region_4.4_spmd, %region_5.7_spmd} | conditional | flops 274467840 | bytes 7931432 | solution.py:91
  57.2 0.5 bitcast_reduce_fusion
  57.7 0.8 %fusion.5 = f32[128,1,8,128]{0,3,2,1:T(8,128)S(1)} fusion(f32[512,128,8]{1,0,2:T(8,128)S(1)} %get-tuple-element.322, f32[8,128]{1,0:T(8,128)S(1)} %bitcast.91, pred[512]{0:T(512)(128)(4,1)S(1)} %get-tuple-element.204, f32[128,1,8,128]{0,3,2,1:T(8,128)S(1)} %get-tuple-element.209, f32[128,8]{0,1:T(8,128)S(1)} %get-tuple-element.317, ...), kind=kOutput, calls=%fused_computation.8 | convolution fusion | flops 136577024 | bytes 3285508 | tf_op jit(solution)/shard_map/while/body/eval_jaxpr/cond/branch_1_fun/kgts,skd->tkgd/dot_general | solution.py:81
  58.5 0.5 fusion.4
  59.0 0.6 dynamic_slice.43
  60.4 0.6 fusion.39
  61.6 1.9 %conditional.3 = ((f32[1,8,128]{2,1,0:T(8,128)S(1)}, f32[1,8,128]{2,1,0:T(8,128)S(1)}, f32[128,1,8,128]{0,3,2,1:T(8,128)S(1)})) conditional(s32[]{:T(128)} %convert_element_type.23, (f32[1,8,128]{2,1,0:T(8,128)S(1)}, f32[1,8,128]{2,1,0:T(8,128)S(1)}, f32[128,1,8,128]{0,3,2,1:T(8,128)S(1)}) %tuple.58, (pred[512]{0:T(512)(128)(4,1)S(1)}, ...), branch_computations={%region_4.4_spmd, %region_5.7_spmd} | conditional | flops 274467840 | bytes 7931432 | solution.py:91
  62.1 0.8 %fusion.5 = f32[128,1,8,128]{0,3,2,1:T(8,128)S(1)} fusion(f32[512,128,8]{1,0,2:T(8,128)S(1)} %get-tuple-element.322, f32[8,128]{1,0:T(8,128)S(1)} %bitcast.91, pred[512]{0:T(512)(128)(4,1)S(1)} %get-tuple-element.204, f32[128,1,8,128]{0,3,2,1:T(8,128)S(1)} %get-tuple-element.209, f32[128,8]{0,1:T(8,128)S(1)} %get-tuple-element.317, ...), kind=kOutput, calls=%fused_computation.8 | convolution fusion | flops 136577024 | bytes 3285508 | tf_op jit(solution)/shard_map/while/body/eval_jaxpr/cond/branch_1_fun/kgts,skd->tkgd/dot_general | solution.py:81
  62.9 0.5 fusion.4
  63.5 0.9 %copy.35 = bf16[128,1024]{1,0:T(8,128)(2,1)} copy(bf16[128,1024]{0,1:T(8,128)(2,1)S(1)} %bitcast.93) | data formatting | bytes 524288 | tf_op jit(solution)/shard_map/reshape | solution.py:105
  (22 shorter events, 1.1 us)
Async XLA Ops:
  0.0 0.8 %copy-start = (bf16[32,512]{1,0:T(8,128)(2,1)S(1)}, bf16[32,512]{1,0:T(8,128)(2,1)}, u32[]{:S(2)}) copy-start(bf16[32,512]{1,0:T(8,128)(2,1)} %param.11) | copy-start | bytes 98308
  0.8 53.8 %copy-start.1 = (s32[8]{0:T(128)S(1)}, s32[8]{0:T(128)}, u32[]{:S(2)}) copy-start(s32[8]{0:T(128)} %param.13) | copy-start | bytes 100
  1.4 7.2 %all-to-all-start.2 = ((bf16[32,4,128]{2,0,1:T(8,128)(2,1)}), bf16[32,4,128]{2,0,1:T(8,128)(2,1)S(1)}, u32[]{:S(2)}, u32[]{:S(2)}) async-start(bf16[32,4,128]{2,0,1:T(8,128)(2,1)} %copy_bitcast_fusion), calls=%async_computation.2 | async-start | bytes 65536 | tf_op jit(solution)/shard_map/all_to_all | solution.py:112
  15.6 38.9 %all-to-all-start.1 = ((bf16[8,128,128]{2,1,0:T(8,128)(2,1)}), bf16[8,128,128]{2,1,0:T(8,128)(2,1)S(1)}, u32[]{:S(2)}, u32[]{:S(2)}) async-start(bf16[8,128,128]{2,1,0:T(8,128)(2,1)} %stack.5), calls=%async_computation.1 | async-start | bytes 524288 | tf_op jit(solution)/shard_map/all_to_all | solution.py:14
